TPU v7x, 32 devices: a whole 2x2x4 slice. The times are simulated.
32 devices in a mesh: ctx: 8 (over y, x, core), ch: 4 (over z).
Axes of the slice: x: 2, y: 2, z: 4, core: 2. Of those that a mesh axis runs over, the one named last changes fastest.
Arguments:
- query_gate: bfloat16 [2048, 4096], P('ctx', 'ch'), may hold values from -6 to 6
- key_gate: bfloat16 [2048, 4096], P('ctx', 'ch'), may hold values from -6 to 6
- values: bfloat16 [2048, 4096], P('ctx', 'ch'), may hold values from -6 to 6
- decay_rates: float32 [16, 4096], P(None, 'ch'), may hold values from 0 to 0.04, as said below
- residues: float32 [16, 4096], P(None, 'ch'), may hold values from -3 to 3
- skip_gain: float32 [4096], P('ch'), may hold values from 0.5 to 1.5
- out_weight: bfloat16 [4096, 4096], P(None, 'ch'), may hold values from -0.09375 to 0.09375
Outputs:
- layer_out: bfloat16 [2048, 4096], P('ctx', 'ch')
- final_state: float32 [16, 4096], P(None, ('ctx', 'ch'))
Inputs may be any that keep to these rules, and one draw needn't show every extreme that they name: `decay_rates`: decay rates are positive.
All inputs are finite; a program needn't handle non-finite values.
Results may differ from a plain program's by a relative error of at most 0.0057.
Values may be sent and summed in bfloat16 or wider, within the bound.
A program may use at most 192 MiB of HBM per device.

v0:
```python
import jax
import jax.numpy as jnp
from jax import lax
from jax.sharding import PartitionSpec as P

BLOCK = 128


def from_root(block, axis, holder):
    block = jnp.where(lax.axis_index(axis) == holder, block, jnp.zeros_like(block))
    return lax.psum(block, axis)


def body(query_gate, key_gate, values, decay_rates, residues, skip_gain, out_weight):
    highest = lax.Precision.HIGHEST
    tokens = values.shape[0]
    channels = values.shape[1]
    block_len = BLOCK
    block_count = tokens // block_len
    gated = (key_gate.astype(jnp.float32) * values.astype(jnp.float32)).astype(jnp.bfloat16)
    upcast = gated.astype(jnp.float32).reshape(block_count, block_len, channels)
    amplitude = residues * jnp.sqrt(-jnp.expm1(-2.0 * decay_rates))
    positions = jnp.arange(block_len).astype(jnp.float32)
    powers = jnp.exp(-decay_rates[None, :, :] * positions[:, None, None])
    taps = jnp.sum(amplitude[None, :, :] * powers, axis=1)
    offset = jnp.arange(block_len)[:, None] - jnp.arange(block_len)[None, :]
    toeplitz = jnp.where((offset >= 0)[:, :, None], taps[jnp.clip(offset, 0, block_len - 1)], 0.0)
    near_part = jnp.einsum("ijc,bjc->bic", toeplitz, upcast, precision=highest)
    end_decay = jnp.exp(-decay_rates[None, :, :] * (block_len - 1.0 - positions)[:, None, None])
    block_states = jnp.einsum("bjc,jmc->bmc", upcast, end_decay, precision=highest)
    targets = jnp.arange(block_count + 1)
    sources = jnp.arange(block_count)
    lag_blocks = targets[:, None] - 1 - sources[None, :]
    lag_float = jnp.maximum(lag_blocks, 0).astype(jnp.float32)
    weights_in = jnp.where(
        (lag_blocks >= 0)[:, :, None, None],
        jnp.exp(-decay_rates[None, None, :, :] * (block_len * lag_float)[:, :, None, None]),
        0.0,
    )
    local_in = jnp.sum(weights_in * block_states[None], axis=1)
    own_state = local_in[block_count]
    every_state = lax.all_gather(own_state[None], "ctx", axis=0, tiled=True)
    ctx_count = lax.axis_size("ctx")
    ctx_here = lax.axis_index("ctx")
    shard_pos = jnp.arange(ctx_count)
    lag_in = ctx_here - 1 - shard_pos
    lag_in_float = jnp.maximum(lag_in, 0).astype(jnp.float32)
    weight_prior = jnp.where(
        (lag_in >= 0)[:, None, None],
        jnp.exp(-decay_rates[None] * (float(tokens) * lag_in_float)[:, None, None]),
        0.0,
    )
    incoming = jnp.sum(weight_prior * every_state, axis=0)
    lag_end = (ctx_count - 1 - shard_pos).astype(jnp.float32)
    total = jnp.sum(
        jnp.exp(-decay_rates[None] * (float(tokens) * lag_end)[:, None, None]) * every_state, axis=0
    )
    start_decay = jnp.exp(
        -decay_rates[None]
        * (block_len * jnp.arange(block_count).astype(jnp.float32))[:, None, None]
    )
    block_in = start_decay * incoming[None] + local_in[:block_count]
    lead_decay = amplitude[None] * jnp.exp(-decay_rates[None] * (positions + 1.0)[:, None, None])
    far_part = jnp.einsum("imc,bmc->bic", lead_decay, block_in, precision=highest)
    convolved = (near_part + far_part).reshape(tokens, channels) + skip_gain[
        None, :
    ] * gated.astype(jnp.float32)
    mixing = (query_gate.astype(jnp.float32) * convolved).astype(jnp.bfloat16)
    projected = jnp.dot(
        lax.all_gather(mixing, "ch", axis=1, tiled=True),
        out_weight,
        preferred_element_type=jnp.float32,
    )
    layer_out = projected.astype(jnp.bfloat16)
    ctx_total = lax.axis_size("ctx")
    groups = lax.axis_size("ch")
    slice_width = channels // ctx_total
    ctx_row = lax.axis_index("ctx")
    root_index = ctx_row * groups // ctx_total
    first_col = ctx_row * groups % ctx_total * slice_width
    scaled = amplitude * total
    row_part = lax.dynamic_slice_in_dim(scaled, first_col, groups * slice_width, 1)
    shared = from_root(row_part, "ch", root_index)
    final_state = lax.dynamic_slice_in_dim(
        shared, lax.axis_index("ch") * slice_width, slice_width, 1
    )
    return (layer_out, final_state)


def solution(mesh):
    return jax.shard_map(
        body,
        mesh=mesh,
        in_specs=(
            P("ctx", "ch"),
            P("ctx", "ch"),
            P("ctx", "ch"),
            P(None, "ch"),
            P(None, "ch"),
            P("ch"),
            P(None, "ch"),
        ),
        out_specs=(P("ctx", "ch"), P(None, ("ctx", "ch"))),
        check_vma=False,
    )
```

profile of v0, /device:TPU:0, one launch (start us, length us, event | category | flops | bytes accessed | tf_op | source)
XLA Modules:
  0.0 322.2 jit_solution(946350587117281502)
XLA Ops:
  7.2 0.0 all-gather.2.cloned.1.call-start
  7.3 0.6 subtract_compare_fusion
  7.9 0.5 broadcast_subtract_fusion
  8.4 0.7 convert_multiply_fusion
  9.1 0.6 fusion.30
  9.7 0.6 convert_multiply_fusion.1
  10.3 0.6 fusion.31
  10.9 0.5 convert_multiply_fusion.3
  11.4 0.5 broadcast_add_fusion
  11.9 1.4 multiply_convert_fusion
  13.3 0.0 copy-start
  13.3 1.1 copy.57
  14.4 0.9 sqrt_multiply_fusion
  15.4 0.2 copy.54
  15.6 0.4 copy-done.11
  16.0 0.2 copy.53
  16.2 11.8 %multiply_reduce_fusion = f32[128,1024]{0,1:T(8,128)S(1)} fusion(f32[128]{0:T(128)S(1)} %iota_convert_fusion, f32[16,1024]{0,1:T(8,128)S(1)} %copy.54, f32[16,1024]{0,1:T(8,128)S(1)} %copy.53), kind=kLoop, calls=%fused_computation.12 | loop fusion | flops 6160384 | bytes 655872 | tf_op jit(solution)/shard_map/reduce_sum | solution.py:25
  28.0 0.2 copy.55
  28.2 71.2 %gather_fusion = f32[16384,1024]{1,0:T(8,128)} fusion(f32[128,1024]{1,0:T(8,128)S(1)} %copy.55, s32[16384]{0:T(1024)S(1)} %fusion.28), kind=kCustom, calls=%fused_computation | custom fusion | bytes 134283264 | tf_op jit(solution)/shard_map/gather | solution.py:27
  99.4 0.0 copy-done.6
  99.4 0.0 copy-start.2
  99.4 0.0 copy-start.7
  99.4 0.0 copy-start.22
  99.4 70.5 %copy.56 = f32[128,128,1024]{1,0,2:T(8,128)} copy(f32[128,128,1024]{2,1,0:T(8,128)} %bitcast.2) | data formatting | bytes 134217728 | tf_op jit(solution)/shard_map/gather | solution.py:27
  169.9 0.0 copy-done.2
  169.9 0.0 copy-done.22
  169.9 0.0 copy-start.14
  170.0 8.3 %fusion.16 = f32[2,16,1024]{1,0,2:T(2,128)S(1)} fusion(bf16[2,128,1024]{1,0,2:T(2,128)(2,1)S(1)} %copy-done.2, f32[128]{0:T(128)S(1)} %copy-done.22, f32[16,1024]{0,1:T(8,128)S(1)} %copy-done.7), kind=kOutput, calls=%fused_computation.18 | convolution fusion | flops 52428800 | bytes 721408 | tf_op jit(solution)/shard_map/bjc,jmc->bmc/dot_general | solution.py:30
  178.2 0.4 copy.59
  178.7 0.1 multiply_reduce_fusion.3
  178.9 11.5 %all_gather.6 = f32[8,16,1024]{2,1,0:T(8,128)S(1)} all-gather(f32[1,16,1024]{2,1,0:T(8,128)S(1)} %slice.10), channel_id=1, replica_groups=mesh['ctx'=8,'ch'=4] {'ctx'}, dimensions={0}, use_global_device_ids=true | all-gather | bytes 589824 | tf_op jit(solution)/shard_map/all_gather | solution.py:42
  190.4 0.0 copy-done.20
  190.4 0.3 multiply_reduce_fusion.1
  190.7 0.1 slice_add_fusion
  190.8 0.5 copy.60
  191.4 57.2 %fusion = f32[1024,2,128]{2,1,0:T(2,128)S(1)} fusion(bf16[2,128,1024]{1,0,2:T(2,128)(2,1)S(1)} %copy-done.2, f32[128,128,1024]{1,0,2:T(8,128)} %copy.56, pred[128,128]{1,0:T(8,128)(4,1)S(1)} %copy-done.13), kind=kOutput, calls=%fused_computation.1 | convolution fusion | flops 419430400 | bytes 68698112 | tf_op jit(solution)/shard_map/ijc,bjc->bic/dot_general | solution.py:28
  248.6 0.0 copy-done.10
  248.6 0.0 copy-done.21
  248.6 0.0 copy-start.5
  248.7 0.0 copy-start.15
  248.7 11.4 %fusion.22 = f32[2,128,1024]{1,0,2:T(2,128)S(1)} fusion(f32[1024,2,128]{2,1,0:T(2,128)S(1)} %fusion, f32[2,16,1024]{1,0,2:T(2,128)S(1)} %copy.60, f32[128]{0:T(128)S(1)} %copy-done.21, f32[16,1024]{0,1:T(8,128)S(1)} %copy-done.8, f32[16,1024]{0,1:T(8,128)S(1)} %copy-done.10), kind=kOutput, calls=%fused_computation.20 | convolution fusion | flops 54788096 | bytes 2359808 | tf_op jit(solution)/shard_map/imc,bmc->bic/dot_general | solution.py:64
  260.1 0.5 copy.64
  260.6 1.0 fusion.26
  261.7 0.0 all-gather.2.cloned.1.call-update
  261.7 20.3 %psum.7 = f32[16,512]{1,0:T(8,128)S(1)} all-reduce(f32[16,512]{1,0:T(8,128)S(1)} %fusion.29), channel_id=1, replica_groups=mesh['ctx'=8,'ch'=4] {'ch'}, use_global_device_ids=true, to_apply=%region_4.5 | all-reduce | flops 8192 | bytes 65536 | tf_op jit(solution)/shard_map/psum | solution.py:11
  282.0 0.6 constant_dynamic-slice_fusion
  282.6 25.6 %all-gather.2.cloned.1.call-done = bf16[256,4096]{1,0:T(8,128)(2,1)} async-done(((bf16[256,1024]{1,0:T(8,128)(2,1)}), bf16[256,4096]{1,0:T(8,128)(2,1)}) %all-gather.2.cloned.1.call-update) | async-done | bytes 2097168 | tf_op jit(solution)/shard_map/all_gather | solution.py:70
  308.2 7.1 %convolution_convert_fusion = bf16[256,1024]{1,0:T(8,128)(2,1)} fusion(bf16[256,4096]{1,0:T(8,128)(2,1)} %all-gather.2.cloned.1.call-done, bf16[4096,1024]{1,0:T(8,128)(2,1)} %param.13), kind=kOutput, calls=%fused_computation.21 | convolution fusion | flops 2147745792 | bytes 11010048 | tf_op jit(solution)/shard_map/dot_general | solution.py:69
  (37 shorter events, 0.1 us)
Async XLA Ops:
  7.2 301.1 %all-gather.2.cloned.1.call-start = ((), (), s32[]{:S(2)}) async-start(), calls=%async_computation | async-start | bytes 2621440 | tf_op jit(solution)/shard_map/all_gather | solution.py:70
  13.3 2.9 copy-start
  15.3 0.6 copy-start.11
  15.3 84.0 %copy-start.3 = (f32[16,1024]{1,0:T(8,128)}, f32[16,1024]{1,0:T(8,128)S(1)}, u32[]{:S(2)}) copy-start(f32[16,1024]{1,0:T(8,128)S(1)} %get-tuple-element.9) | copy-start | bytes 196612
  15.6 83.8 %copy-start.6 = (f32[16,1024]{0,1:T(8,128)}, f32[16,1024]{0,1:T(8,128)S(1)}, u32[]{:S(2)}) copy-start(f32[16,1024]{0,1:T(8,128)S(1)} %copy.54) | copy-start | bytes 196612
  16.2 83.2 %copy-start.9 = (f32[16,1024]{0,1:T(8,128)}, f32[16,1024]{0,1:T(8,128)S(1)}, u32[]{:S(2)}) copy-start(f32[16,1024]{0,1:T(8,128)S(1)} %copy.53) | copy-start | bytes 196612
  99.4 70.5 %copy-start.2 = (bf16[2,128,1024]{1,0,2:T(2,128)(2,1)S(1)}, bf16[2,128,1024]{1,0,2:T(2,128)(2,1)}, u32[]{:S(2)}) copy-start(bf16[2,128,1024]{1,0,2:T(2,128)(2,1)} %copy.57) | copy-start | bytes 1572868
  99.4 70.5 %copy-start.7 = (f32[16,1024]{0,1:T(8,128)S(1)}, f32[16,1024]{0,1:T(8,128)}, u32[]{:S(2)}) copy-start(f32[16,1024]{0,1:T(8,128)} %copy-done.6) | copy-start | bytes 196612
  99.4 70.5 %copy-start.22 = (f32[128]{0:T(128)S(1)}, f32[128]{0:T(128)}, u32[]{:S(2)}) copy-start(f32[128]{0:T(128)} %broadcast_subtract_fusion) | copy-start | bytes 1540
  169.9 8.8 %copy-start.4 = (f32[16,1024]{1,0:T(8,128)S(1)}, f32[16,1024]{1,0:T(8,128)}, u32[]{:S(2)}) copy-start(f32[16,1024]{1,0:T(8,128)} %copy-done.3) | copy-start | bytes 196612
  169.9 8.8 %copy-start.14 = (f32[3,2]{1,0:T(4,128)S(1)}, f32[3,2]{1,0:T(4,128)}, u32[]{:S(2)}) copy-start(f32[3,2]{1,0:T(4,128)} %convert_multiply_fusion) | copy-start | bytes 76
  169.9 8.8 %copy-start.16 = (pred[3,2]{1,0:T(4,128)(4,1)S(1)}, pred[3,2]{1,0:T(4,128)(4,1)}, u32[]{:S(2)}) copy-start(pred[3,2]{1,0:T(4,128)(4,1)} %fusion.30) | copy-start | bytes 22
  169.9 20.5 %copy-start.18 = (f32[8]{0:T(128)S(1)}, f32[8]{0:T(128)}, u32[]{:S(2)}) copy-start(f32[8]{0:T(128)} %get-tuple-element.10) | copy-start | bytes 100
  169.9 20.4 %copy-start.19 = (f32[8]{0:T(128)S(1)}, f32[8]{0:T(128)}, u32[]{:S(2)}) copy-start(f32[8]{0:T(128)} %get-tuple-element.11) | copy-start | bytes 100
  169.9 20.4 %copy-start.20 = (pred[8]{0:T(512)(128)(4,1)S(1)}, pred[8]{0:T(512)(128)(4,1)}, u32[]{:S(2)}) copy-start(pred[8]{0:T(512)(128)(4,1)} %fusion.31) | copy-start | bytes 28
  169.9 20.8 %copy-start.17 = (f32[2]{0:T(128)S(1)}, f32[2]{0:T(128)}, u32[]{:S(2)}) copy-start(f32[2]{0:T(128)} %convert_multiply_fusion.3) | copy-start | bytes 28
  170.0 21.4 %copy-start.13 = (pred[128,128]{1,0:T(8,128)(4,1)S(1)}, pred[128,128]{1,0:T(8,128)(4,1)}, u32[]{:S(2)}) copy-start(pred[128,128]{1,0:T(8,128)(4,1)} %subtract_compare_fusion) | copy-start | bytes 49156
  191.4 57.2 %copy-start.8 = (f32[16,1024]{0,1:T(8,128)S(1)}, f32[16,1024]{0,1:T(8,128)}, u32[]{:S(2)}) copy-start(f32[16,1024]{0,1:T(8,128)} %copy-done.6) | copy-start | bytes 196612
  191.4 57.2 %copy-start.10 = (f32[16,1024]{0,1:T(8,128)S(1)}, f32[16,1024]{0,1:T(8,128)}, u32[]{:S(2)}) copy-start(f32[16,1024]{0,1:T(8,128)} %copy-done.9) | copy-start | bytes 196612
  191.4 57.2 %copy-start.21 = (f32[128]{0:T(128)S(1)}, f32[128]{0:T(128)}, u32[]{:S(2)}) copy-start(f32[128]{0:T(128)} %broadcast_add_fusion) | copy-start | bytes 1540
  248.6 11.9 %copy-start.1 = (bf16[256,1024]{1,0:T(8,128)(2,1)S(1)}, bf16[256,1024]{1,0:T(8,128)(2,1)}, u32[]{:S(2)}) copy-start(bf16[256,1024]{1,0:T(8,128)(2,1)} %copy-done) | copy-start | bytes 1572868
  248.6 11.9 %copy-start.5 = (bf16[256,1024]{1,0:T(8,128)(2,1)S(1)}, bf16[256,1024]{1,0:T(8,128)(2,1)}, u32[]{:S(2)}) copy-start(bf16[256,1024]{1,0:T(8,128)(2,1)} %param.7) | copy-start | bytes 1572868
  248.7 11.9 %copy-start.15 = (f32[1024]{0:T(1024)S(1)}, f32[1024]{0:T(1024)}, u32[]{:S(2)}) copy-start(f32[1024]{0:T(1024)} %param.12) | copy-start | bytes 12292
  248.7 13.0 %copy-start.12 = (f32[16,1024]{1,0:T(8,128)S(1)}, f32[16,1024]{1,0:T(8,128)}, u32[]{:S(2)}) copy-start(f32[16,1024]{1,0:T(8,128)} %copy-done.11) | copy-start | bytes 196612
Sparse Core Ops, SparseCore 0:
  261.8 46.3 all-gather.1
where the time goes:
time: 323 us; the launch traced here: 322 us
  local copies, waits for them, and re-layouts  146 us (45%)
  matrix products  83.9 us (26%)
  blocking collectives  31.8 us (10%)
  waiting for transfers between devices  25.6 us (8%)
  other arithmetic  20.4 us (6%)
  between operations  14.5 us (4%)
    gather x2, local copies, waits for them, and re-layouts, body(): taps[jnp.clip(offset, 0, block_len - 1)]  142 us
    dot_general x1, matrix products, body(): near_part = jnp.einsum('ijc,bjc->bic', toeplitz, upcast, precision=highest)  57.2 us
    all_gather x1, waiting for transfers between devices, body(): lax.all_gather(mixing, 'ch', axis=1, tiled=True)  25.6 us
    psum x1, blocking collectives, from_root(): return lax.psum(block, axis)  20.3 us
    reduce_sum x1, other arithmetic, body(): taps = jnp.sum(amplitude[None, :, :] * powers, axis=1)  11.8 us
    all_gather x1, blocking collectives, body(): every_state = lax.all_gather(own_state[None], 'ctx', axis=0, tiled=True)  11.5 us
    dot_general x1, matrix products, body(): jnp.einsum('imc,bmc->bic', lead_decay, block_in, precision=highest)  11.4 us
    dot_general x1, matrix products, body(): jnp.einsum('bjc,jmc->bmc', upcast, end_decay, precision=highest)  8.25 us
  transfers between devices with their start and end apart: 1, of which 1 were waited for; matrix products, arithmetic and copies ran while one was open for 0% of the time, Pallas kernels for 0%

commit v1 on v0

v1 whole, which is shorter than its diff:
```python
import functools

import jax
import jax.numpy as jnp
from jax import lax
from jax.experimental import pallas as pl
from jax.experimental.pallas import tpu as pltpu
from jax.sharding import PartitionSpec as P

LANES = 128
SEGS = 8
CHUNK = 256
MESH = pl.DeviceIdType.MESH


def one_minus_exp(z):
    series = 1.0 - z * (1.0 / 8.0)
    for k in (7.0, 6.0, 5.0, 4.0, 3.0, 2.0):
        series = 1.0 - z * (1.0 / k) * series
    return jnp.where(z < 0.25, z * series, 1.0 - jnp.exp(-z))


def kernel(
    ctx_count, groups, chunk, fin_width, fin_stride,
    q_hbm, k_hbm, v_hbm, rate_ref, res_ref, skip_ref, w_hbm,
    out_ref, fin_ref,
    qb, kb, vb, wb, ub, yb, qp, mix, acc, states, seed_in, seed_pow, inc, final_row, final_got,
    perm, perm_back,
    load_sem, w_sem, st_send, st_recv, mx_send, mx_recv, fin_send, fin_recv,
):
    rows, channels = qb.shape
    poles = rate_ref.shape[0]
    steps = rows // SEGS
    chunks = channels // chunk
    tiles = chunk // LANES
    me = lax.axis_index("ctx")
    here = lax.axis_index("ch")

    loads = []
    for c in range(chunks):
        sl = pl.ds(c * chunk, chunk)
        group = []
        for n, (src, dst) in enumerate(((k_hbm, kb), (v_hbm, vb), (q_hbm, qb))):
            copy = pltpu.make_async_copy(src.at[:, sl], dst.at[:, sl], load_sem.at[n, c])
            copy.start()
            group.append(copy)
        loads.append(group)
    w_copy = pltpu.make_async_copy(w_hbm, wb, w_sem)
    w_copy.start()

    barrier = pltpu.get_barrier_semaphore()
    for d in range(1, ctx_count):
        pl.semaphore_signal(
            barrier, inc=1, device_id={"ctx": lax.rem(me + d, ctx_count)}, device_id_type=MESH
        )
    for d in range(1, groups):
        pl.semaphore_signal(
            barrier, inc=1, device_id={"ch": lax.rem(here + d, groups)}, device_id_type=MESH
        )

    first = lax.broadcasted_iota(jnp.int32, (rows, rows), 0)
    second = lax.broadcasted_iota(jnp.int32, (rows, rows), 1)
    perm[...] = jnp.where(second == (first % SEGS) * steps + first // SEGS, 1.0, 0.0).astype(jnp.bfloat16)
    perm_back[...] = jnp.where(first == (second % SEGS) * steps + second // SEGS, 1.0, 0.0).astype(jnp.bfloat16)

    def spread(ref, lane):
        return jnp.stack(
            [jnp.broadcast_to(ref[m : m + 1, pl.ds(lane, LANES)], (SEGS, LANES)) for m in range(poles)]
        )

    seg = lax.broadcasted_iota(jnp.int32, (poles, SEGS, LANES), 1)

    def state_copy(slot, peer, c):
        sl = pl.ds(c * chunk, chunk)
        return pltpu.make_async_remote_copy(
            src_ref=states.at[slot, :, sl],
            dst_ref=states.at[slot, :, sl],
            send_sem=st_send.at[peer, c],
            recv_sem=st_recv.at[slot, c],
            device_id={"ctx": peer},
            device_id_type=MESH,
        )

    for c in range(chunks):
        sl = pl.ds(c * chunk, chunk)
        for copy in loads[c]:
            copy.wait()
        gated = (kb[:, sl].astype(jnp.float32) * vb[:, sl].astype(jnp.float32)).astype(jnp.bfloat16)
        ub[:, sl] = jnp.dot(perm[...], gated, preferred_element_type=jnp.float32)

        @pl.loop(0, tiles)
        def _(t):
            lane = pl.multiple_of(c * chunk + t * LANES, LANES)
            tl = pl.ds(lane, LANES)
            rate = spread(rate_ref, lane)
            amp = spread(res_ref, lane) * jnp.sqrt(one_minus_exp(2.0 * rate))
            pole = jnp.exp(-rate)
            skip = jnp.broadcast_to(skip_ref[0:1, tl], (SEGS, LANES))

            def step(i, x):
                at = pl.ds(pl.multiple_of(i * SEGS, SEGS), SEGS)
                u = ub[at, tl]
                x = pole * x + u[None]
                yb[at, tl] = jnp.sum(amp * x, axis=0) + skip * u
                return x

            x = lax.fori_loop(0, steps, step, jnp.zeros((poles, SEGS, LANES), jnp.float32), unroll=4)
            span = 1
            while span < SEGS:
                weight = jnp.where(seg >= span, jnp.exp(rate * (-1.0 * steps * span)), 0.0)
                x = x + weight * pltpu.roll(x, span, 1)
                span *= 2
            for m in range(poles):
                states[me, m : m + 1, tl] = x[m, SEGS - 1 : SEGS]
            before = jnp.where(seg >= 1, pltpu.roll(x, 1, 1), 0.0)
            seed_in[:, :, tl] = amp * before
            seed_pow[:, :, tl] = amp * jnp.exp(rate * (seg.astype(jnp.float32) * (-1.0 * steps)))

        if c == 0:
            pl.semaphore_wait(barrier, ctx_count - 1 + groups - 1)
        for d in range(1, ctx_count):
            state_copy(me, lax.rem(me + d, ctx_count), c).start()

    for c in range(chunks):
        sl = pl.ds(c * chunk, chunk)
        qp[:, sl] = jnp.dot(perm[...], qb[:, sl], preferred_element_type=jnp.float32)

    def mix_copy(owner, c, way):
        sl = pl.ds(pl.multiple_of(c * chunk, chunk), chunk)
        return pltpu.make_async_remote_copy(
            src_ref=mix.at[owner, :, sl],
            dst_ref=mix.at[owner, :, sl],
            send_sem=mx_send.at[way, owner, c],
            recv_sem=mx_recv.at[owner, c],
            device_id={"ch": here + 1 if way else here - 1},
            device_id_type=MESH,
        )

    has_right = here < groups - 1
    has_left = here > 0

    for c in range(chunks):
        sl = pl.ds(c * chunk, chunk)
        for d in range(1, ctx_count):
            state_copy(lax.rem(me + d, ctx_count), me, c).wait_recv()
        rate = rate_ref[:, sl]
        across = jnp.exp(rate * (-1.0 * rows))
        total = jnp.zeros_like(rate)
        incoming = jnp.zeros_like(rate)
        for j in range(ctx_count):
            incoming = jnp.where(me == j, total, incoming)
            total = total * across + states[j, :, sl]
        inc[:, sl] = incoming
        final_row[:, sl] = res_ref[:, sl] * jnp.sqrt(one_minus_exp(2.0 * rate)) * total

        @pl.loop(0, tiles)
        def _(t):
            lane = pl.multiple_of(c * chunk + t * LANES, LANES)
            tl = pl.ds(lane, LANES)
            pole = jnp.exp(-spread(rate_ref, lane))
            carry = seed_in[:, :, tl] + seed_pow[:, :, tl] * spread(inc, lane)

            def step(i, x):
                at = pl.ds(pl.multiple_of(i * SEGS, SEGS), SEGS)
                x = pole * x
                yb[at, tl] += jnp.sum(x, axis=0)
                return x

            lax.fori_loop(0, steps, step, carry, unroll=4)

        mixing = (qp[:, sl] * yb[:, sl]).astype(jnp.bfloat16)
        mix[here, :, sl] = jnp.dot(
            perm_back[...], mixing, preferred_element_type=jnp.float32
        ).astype(jnp.bfloat16)

        @pl.when(has_right)
        def _():
            mix_copy(here, c, 1).start()

        @pl.when(has_left)
        def _():
            mix_copy(here, c, 0).start()

    root = me * groups // ctx_count
    first_col = lax.rem(me * groups, ctx_count) * (channels // ctx_count)

    def final_copy(peer):
        return pltpu.make_async_remote_copy(
            src_ref=final_row.at[:, pl.ds(pl.multiple_of(first_col + peer * fin_stride, LANES), fin_width)],
            dst_ref=final_got,
            send_sem=fin_send.at[peer],
            recv_sem=fin_recv,
            device_id={"ch": peer},
            device_id_type=MESH,
        )

    @pl.when(here == root)
    def _():
        for d in range(1, groups):
            final_copy(lax.rem(here + d, groups)).start()

    w_copy.wait()

    def project(owner, c):
        at = pl.multiple_of(c * chunk, chunk)
        return jnp.dot(
            mix[owner, :, pl.ds(at, chunk)],
            wb[pl.ds(pl.multiple_of(owner * channels + at, chunk), chunk), :],
            preferred_element_type=jnp.float32,
        )

    acc[...] = project(here, 0)
    if chunks > 1:
        @pl.loop(1, chunks)
        def _(c):
            acc[...] += project(here, c)

    @pl.loop(0, (groups - 1) * chunks)
    def _(n):
        d = 1 + n // chunks
        c = n % chunks
        left = here - d
        right = here + d

        @pl.when(left >= 0)
        def _():
            mix_copy(left, c, 1).wait_recv()

            @pl.when(has_right)
            def _():
                mix_copy(left, c, 1).start()

        @pl.when(right < groups)
        def _():
            mix_copy(right, c, 0).wait_recv()

            @pl.when(has_left)
            def _():
                mix_copy(right, c, 0).start()

        @pl.when(left >= 0)
        def _():
            acc[...] += project(left, c)

        @pl.when(right < groups)
        def _():
            acc[...] += project(right, c)

    out_ref[...] = acc[...].astype(jnp.bfloat16)

    @pl.when(here == root)
    def _():
        fin_ref[...] = final_row[:, pl.ds(pl.multiple_of(first_col + here * fin_stride, LANES), fin_width)]
        for d in range(1, groups):
            final_copy(lax.rem(here + d, groups)).wait_send()

    @pl.when(here != root)
    def _():
        final_copy(here).wait_recv()
        fin_ref[...] = final_got[...]

    for c in range(chunks):
        for d in range(1, ctx_count):
            state_copy(me, lax.rem(me + d, ctx_count), c).wait_send()

    @pl.loop(0, groups * chunks)
    def _(n):
        owner = n // chunks
        c = n % chunks

        @pl.when(jnp.logical_and(owner <= here, has_right))
        def _():
            mix_copy(owner, c, 1).wait_send()

        @pl.when(jnp.logical_and(owner >= here, has_left))
        def _():
            mix_copy(owner, c, 0).wait_send()


def body(query_gate, key_gate, values, decay_rates, residues, skip_gain, out_weight):
    rows, channels = values.shape
    poles = decay_rates.shape[0]
    ctx_count = lax.axis_size("ctx")
    groups = lax.axis_size("ch")
    chunk = min(CHUNK, channels)
    chunks = channels // chunk
    columns = out_weight.shape[1]
    slice_width = channels // ctx_count
    aligned = slice_width % LANES == 0
    fin_width = slice_width if aligned else groups * slice_width
    fin_stride = slice_width if aligned else 0
    f32, bf16 = jnp.float32, jnp.bfloat16
    dma = pltpu.SemaphoreType.DMA
    any_spec = pl.BlockSpec(memory_space=pl.ANY)
    vmem = pl.BlockSpec(memory_space=pltpu.VMEM)
    layer_out, final = pl.pallas_call(
        functools.partial(kernel, ctx_count, groups, chunk, fin_width, fin_stride),
        out_shape=(
            jax.ShapeDtypeStruct((rows, columns), bf16),
            jax.ShapeDtypeStruct((poles, fin_width), f32),
        ),
        in_specs=[any_spec, any_spec, any_spec, vmem, vmem, vmem, any_spec],
        out_specs=(vmem, vmem),
        scratch_shapes=[
            pltpu.VMEM((rows, channels), bf16),
            pltpu.VMEM((rows, channels), bf16),
            pltpu.VMEM((rows, channels), bf16),
            pltpu.VMEM(out_weight.shape, bf16),
            pltpu.VMEM((rows, channels), f32),
            pltpu.VMEM((rows, channels), f32),
            pltpu.VMEM((rows, channels), f32),
            pltpu.VMEM((groups, rows, channels), bf16),
            pltpu.VMEM((rows, columns), f32),
            pltpu.VMEM((ctx_count, poles, channels), f32),
            pltpu.VMEM((poles, SEGS, channels), f32),
            pltpu.VMEM((poles, SEGS, channels), f32),
            pltpu.VMEM((poles, channels), f32),
            pltpu.VMEM((poles, channels), f32),
            pltpu.VMEM((poles, fin_width), f32),
            pltpu.VMEM((rows, rows), bf16),
            pltpu.VMEM((rows, rows), bf16),
            dma((3, chunks)),
            dma,
            dma((ctx_count, chunks)),
            dma((ctx_count, chunks)),
            dma((2, groups, chunks)),
            dma((groups, chunks)),
            dma((groups,)),
            dma,
        ],
        compiler_params=pltpu.CompilerParams(
            collective_id=0, has_side_effects=True, vmem_limit_bytes=60 * 1024 * 1024
        ),
    )(query_gate, key_gate, values, decay_rates, residues, skip_gain[None, :], out_weight)
    if not aligned:
        final = lax.dynamic_slice_in_dim(final, lax.axis_index("ch") * slice_width, slice_width, 1)
    return layer_out, final


def solution(mesh):
    return jax.shard_map(
        body,
        mesh=mesh,
        in_specs=(
            P("ctx", "ch"),
            P("ctx", "ch"),
            P("ctx", "ch"),
            P(None, "ch"),
            P(None, "ch"),
            P("ch"),
            P(None, "ch"),
        ),
        out_specs=(P("ctx", "ch"), P(None, ("ctx", "ch"))),
        check_vma=False,
    )
```

time: 323 us -> 53.2 us (0.16)
  local copies, waits for them, and re-layouts: 146 us -> 3.16 us
  matrix products: 83.9 us -> 0 us
  Pallas kernels: 0 us -> 49.1 us
  blocking collectives: 31.8 us -> 0 us
  waiting for transfers between devices: 25.6 us -> 0 us
  other arithmetic: 20.4 us -> 0 us
  between operations: 14.5 us -> 0.64 us
    gather x2 -> x0, local copies, waits for them, and re-layouts: 142 us -> none  [body(): taps[jnp.clip(offset, 0, block_len - 1)]]
    dot_general x4 -> x0, matrix products: 83.9 us -> none  [the longest x1 57.2 us: body(): near_part = jnp.einsum('ijc,bjc->bic', toeplitz, upcast, precision=highest)]
    pallas_call x0 -> x1, Pallas kernels: none -> 49.1 us  [body(): pl.pallas_call(functools.partial(kernel, ctx_count, groups, chunk, fin_wi...]
    all_gather x1 -> x0, waiting for transfers between devices: 25.6 us -> none  [body(): lax.all_gather(mixing, 'ch', axis=1, tiled=True)]
    psum x1 -> x0, blocking collectives: 20.3 us -> none  [from_root(): return lax.psum(block, axis)]
    reduce_sum x3 -> x0, other arithmetic: 12.3 us -> none  [the longest x1 11.8 us: body(): taps = jnp.sum(amplitude[None, :, :] * powers, axis=1)]
    all_gather x1 -> x0, blocking collectives: 11.5 us -> none  [body(): every_state = lax.all_gather(own_state[None], 'ctx', axis=0, tiled=True)]
  transfers between devices with their start and end apart: 1 -> 0, of which waited for: 1 -> 0; matrix products, arithmetic and copies ran while one was open for 0% -> 0% of each run, Pallas kernels for 0% -> 0%
where the time goes in v1:
time: 53.2 us; the launch traced here: 52.9 us
  Pallas kernels  49.1 us (92%)
  local copies, waits for them, and re-layouts  3.16 us (6%)
  between operations  0.64 us (1%)
    pallas_call x1, Pallas kernels, body(): pl.pallas_call(functools.partial(kernel, ctx_count, groups, chunk, fin_wi...  49.1 us
    unnamed x2, local copies, waits for them, and re-layouts  3.16 us

profile of v1, /device:TPU:0, one launch (start us, length us, event | category | flops | bytes accessed | tf_op | source)
XLA Modules:
  0.0 52.9 jit_solution(8833355471902362061)
XLA Ops:
  0.6 49.1 %shard_map.86 = (bf16[256,1024]{1,0:T(8,128)(2,1)}, f32[16,128]{1,0:T(8,128)}) custom-call(bf16[256,1024]{1,0:T(8,128)(2,1)} %q_hbm.1, bf16[256,1024]{1,0:T(8,128)(2,1)} %k_hbm.1, bf16[256,1024]{1,0:T(8,128)(2,1)} %v_hbm.1, f32[16,1024]{1,0:T(8,128)} %rate_ref.1, f32[16,1024]{1,0:T(8,128)} %res_ref.1, f32[1,1024]{1,0:T(1,128)} %bitcast.1, ...), custom_call_target="tpu_custom_call" | custom-call | tf_op jit(solution)/shard_map/pallas_call | solution.py:296
  49.8 1.9 %copy.11 = bf16[256,1024]{1,0:T(8,128)(2,1)} copy(bf16[256,1024]{1,0:T(8,128)(2,1)} %get-tuple-element.4) | data formatting | bytes 1048576
  51.6 1.3 %copy.12 = f32[16,128]{1,0:T(8,128)} copy(f32[16,128]{1,0:T(8,128)} %get-tuple-element.5) | data formatting | bytes 16384

commit v2 on v1

--- a/solution.py
+++ b/solution.py
@@ -10,6 +10,7 @@
 LANES = 128
 SEGS = 8
 CHUNK = 256
+AHEAD = 3
 MESH = pl.DeviceIdType.MESH
 
 
@@ -60,8 +61,8 @@
 
     first = lax.broadcasted_iota(jnp.int32, (rows, rows), 0)
     second = lax.broadcasted_iota(jnp.int32, (rows, rows), 1)
-    perm[...] = jnp.where(second == (first % SEGS) * steps + first // SEGS, 1.0, 0.0).astype(jnp.bfloat16)
-    perm_back[...] = jnp.where(first == (second % SEGS) * steps + second // SEGS, 1.0, 0.0).astype(jnp.bfloat16)
+    perm[...] = jnp.where(second == (first & (SEGS - 1)) * steps + (first >> 3), 1.0, 0.0).astype(jnp.bfloat16)
+    perm_back[...] = jnp.where(first == (second & (SEGS - 1)) * steps + (second >> 3), 1.0, 0.0).astype(jnp.bfloat16)
 
     def spread(ref, lane):
         return jnp.stack(
@@ -71,17 +72,16 @@
     seg = lax.broadcasted_iota(jnp.int32, (poles, SEGS, LANES), 1)
 
     def state_copy(slot, peer, c):
-        sl = pl.ds(c * chunk, chunk)
         return pltpu.make_async_remote_copy(
-            src_ref=states.at[slot, :, sl],
-            dst_ref=states.at[slot, :, sl],
+            src_ref=states.at[slot, c],
+            dst_ref=states.at[slot, c],
             send_sem=st_send.at[peer, c],
             recv_sem=st_recv.at[slot, c],
             device_id={"ctx": peer},
             device_id_type=MESH,
         )
 
-    for c in range(chunks):
+    def local(c):
         sl = pl.ds(c * chunk, chunk)
         for copy in loads[c]:
             copy.wait()
@@ -111,7 +111,7 @@
                 x = x + weight * pltpu.roll(x, span, 1)
                 span *= 2
             for m in range(poles):
-                states[me, m : m + 1, tl] = x[m, SEGS - 1 : SEGS]
+                states[me, c, m : m + 1, pl.ds(pl.multiple_of(t * LANES, LANES), LANES)] = x[m, SEGS - 1 : SEGS]
             before = jnp.where(seg >= 1, pltpu.roll(x, 1, 1), 0.0)
             seed_in[:, :, tl] = amp * before
             seed_pow[:, :, tl] = amp * jnp.exp(rate * (seg.astype(jnp.float32) * (-1.0 * steps)))
@@ -120,16 +120,12 @@
             pl.semaphore_wait(barrier, ctx_count - 1 + groups - 1)
         for d in range(1, ctx_count):
             state_copy(me, lax.rem(me + d, ctx_count), c).start()
-
-    for c in range(chunks):
-        sl = pl.ds(c * chunk, chunk)
         qp[:, sl] = jnp.dot(perm[...], qb[:, sl], preferred_element_type=jnp.float32)
 
     def mix_copy(owner, c, way):
-        sl = pl.ds(pl.multiple_of(c * chunk, chunk), chunk)
         return pltpu.make_async_remote_copy(
-            src_ref=mix.at[owner, :, sl],
-            dst_ref=mix.at[owner, :, sl],
+            src_ref=mix.at[owner, c],
+            dst_ref=mix.at[owner, c],
             send_sem=mx_send.at[way, owner, c],
             recv_sem=mx_recv.at[owner, c],
             device_id={"ch": here + 1 if way else here - 1},
@@ -139,7 +135,7 @@
     has_right = here < groups - 1
     has_left = here > 0
 
-    for c in range(chunks):
+    def finish(c):
         sl = pl.ds(c * chunk, chunk)
         for d in range(1, ctx_count):
             state_copy(lax.rem(me + d, ctx_count), me, c).wait_recv()
@@ -149,7 +145,7 @@
         incoming = jnp.zeros_like(rate)
         for j in range(ctx_count):
             incoming = jnp.where(me == j, total, incoming)
-            total = total * across + states[j, :, sl]
+            total = total * across + states[j, c]
         inc[:, sl] = incoming
         final_row[:, sl] = res_ref[:, sl] * jnp.sqrt(one_minus_exp(2.0 * rate)) * total
 
@@ -169,7 +165,7 @@
             lax.fori_loop(0, steps, step, carry, unroll=4)
 
         mixing = (qp[:, sl] * yb[:, sl]).astype(jnp.bfloat16)
-        mix[here, :, sl] = jnp.dot(
+        mix[here, c] = jnp.dot(
             perm_back[...], mixing, preferred_element_type=jnp.float32
         ).astype(jnp.bfloat16)
 
@@ -180,6 +176,12 @@
         @pl.when(has_left)
         def _():
             mix_copy(here, c, 0).start()
+
+    for c in range(chunks + AHEAD):
+        if c < chunks:
+            local(c)
+        if c >= AHEAD:
+            finish(c - AHEAD)
 
     root = me * groups // ctx_count
     first_col = lax.rem(me * groups, ctx_count) * (channels // ctx_count)
@@ -204,7 +206,7 @@
     def project(owner, c):
         at = pl.multiple_of(c * chunk, chunk)
         return jnp.dot(
-            mix[owner, :, pl.ds(at, chunk)],
+            mix[owner, c],
             wb[pl.ds(pl.multiple_of(owner * channels + at, chunk), chunk), :],
             preferred_element_type=jnp.float32,
         )
@@ -275,6 +277,15 @@
         @pl.when(jnp.logical_and(owner >= here, has_left))
         def _():
             mix_copy(owner, c, 0).wait_send()
+
+
+def write_out(out_ref, fin_ref, out_hbm, fin_hbm, sems):
+    first = pltpu.make_async_copy(out_ref, out_hbm, sems.at[0])
+    second = pltpu.make_async_copy(fin_ref, fin_hbm, sems.at[1])
+    first.start()
+    second.start()
+    first.wait()
+    second.wait()
 
 
 def body(query_gate, key_gate, values, decay_rates, residues, skip_gain, out_weight):
@@ -309,9 +320,9 @@
             pltpu.VMEM((rows, channels), f32),
             pltpu.VMEM((rows, channels), f32),
             pltpu.VMEM((rows, channels), f32),
-            pltpu.VMEM((groups, rows, channels), bf16),
+            pltpu.VMEM((groups, chunks, rows, chunk), bf16),
             pltpu.VMEM((rows, columns), f32),
-            pltpu.VMEM((ctx_count, poles, channels), f32),
+            pltpu.VMEM((ctx_count, chunks, poles, chunk), f32),
             pltpu.VMEM((poles, SEGS, channels), f32),
             pltpu.VMEM((poles, SEGS, channels), f32),
             pltpu.VMEM((poles, channels), f32),
@@ -332,6 +343,16 @@
             collective_id=0, has_side_effects=True, vmem_limit_bytes=60 * 1024 * 1024
         ),
     )(query_gate, key_gate, values, decay_rates, residues, skip_gain[None, :], out_weight)
+    layer_out, final = pl.pallas_call(
+        write_out,
+        out_shape=(
+            jax.ShapeDtypeStruct(layer_out.shape, layer_out.dtype),
+            jax.ShapeDtypeStruct(final.shape, final.dtype),
+        ),
+        in_specs=[vmem, vmem],
+        out_specs=(any_spec, any_spec),
+        scratch_shapes=[dma((2,))],
+    )(layer_out, final)
     if not aligned:
         final = lax.dynamic_slice_in_dim(final, lax.axis_index("ch") * slice_width, slice_width, 1)
     return layer_out, final

time: 53.2 us -> 52.1 us (0.979)
  local copies, waits for them, and re-layouts: 3.16 us -> 0 us
  Pallas kernels: 49.1 us -> 51.3 us
    unnamed x2 -> x0, local copies, waits for them, and re-layouts: 3.16 us -> none
    pallas_call x0 -> x1, Pallas kernels: none -> 1.86 us  [body(): pl.pallas_call(write_out, out_shape=(jax.ShapeDtypeStruct(layer_out.shape...]
where the time goes in v2:
time: 52.1 us; the launch traced here: 51.9 us
  Pallas kernels  51.3 us (98%)
  between operations  0.64 us (1%)
    pallas_call x1, Pallas kernels, body(): pl.pallas_call(functools.partial(kernel, ctx_count, groups, chunk, fin_wi...  49.4 us
    pallas_call x1, Pallas kernels, body(): pl.pallas_call(write_out, out_shape=(jax.ShapeDtypeStruct(layer_out.shape...  1.86 us

profile of v2, /device:TPU:0, one launch (start us, length us, event | category | flops | bytes accessed | tf_op | source)
XLA Modules:
  0.0 51.9 jit_solution(8236589815175963013)
XLA Ops:
  0.6 49.4 %shard_map.86 = (bf16[256,1024]{1,0:T(8,128)(2,1)}, f32[16,128]{1,0:T(8,128)}) custom-call(bf16[256,1024]{1,0:T(8,128)(2,1)} %q_hbm.1, bf16[256,1024]{1,0:T(8,128)(2,1)} %k_hbm.1, bf16[256,1024]{1,0:T(8,128)(2,1)} %v_hbm.1, f32[16,1024]{1,0:T(8,128)} %rate_ref.1, f32[16,1024]{1,0:T(8,128)} %res_ref.1, f32[1,1024]{1,0:T(1,128)} %bitcast.1, ...), custom_call_target="tpu_custom_call" | custom-call | tf_op jit(solution)/shard_map/pallas_call | solution.py:307
  50.1 1.9 %shard_map.87 = (bf16[256,1024]{1,0:T(8,128)(2,1)}, f32[16,128]{1,0:T(8,128)}) custom-call(bf16[256,1024]{1,0:T(8,128)(2,1)} %get-tuple-element.4.out_ref, f32[16,128]{1,0:T(8,128)} %get-tuple-element.5.fin_ref), custom_call_target="tpu_custom_call" | custom-call | tf_op jit(solution)/shard_map/pallas_call | solution.py:346

commit v3 on v2

--- a/solution.py
+++ b/solution.py
@@ -10,7 +10,7 @@
 LANES = 128
 SEGS = 8
 CHUNK = 256
-AHEAD = 3
+AHEAD = 1
 MESH = pl.DeviceIdType.MESH
 
 
@@ -47,7 +47,6 @@
             group.append(copy)
         loads.append(group)
     w_copy = pltpu.make_async_copy(w_hbm, wb, w_sem)
-    w_copy.start()
 
     barrier = pltpu.get_barrier_semaphore()
     for d in range(1, ctx_count):
@@ -85,6 +84,8 @@
         sl = pl.ds(c * chunk, chunk)
         for copy in loads[c]:
             copy.wait()
+        if c == 0:
+            w_copy.start()
         gated = (kb[:, sl].astype(jnp.float32) * vb[:, sl].astype(jnp.float32)).astype(jnp.bfloat16)
         ub[:, sl] = jnp.dot(perm[...], gated, preferred_element_type=jnp.float32)
 

time: 52.1 us -> 51.5 us (0.988)
  Pallas kernels: 51.3 us -> 50.7 us
    pallas_call x1, Pallas kernels: 49.4 us -> 48.8 us  [body(): pl.pallas_call(functools.partial(kernel, ctx_count, groups, chunk, fin_wi...]
where the time goes in v3:
time: 51.5 us; the launch traced here: 51.3 us
  Pallas kernels  50.7 us (98%)
  between operations  0.64 us (1%)
    pallas_call x1, Pallas kernels, body(): pl.pallas_call(functools.partial(kernel, ctx_count, groups, chunk, fin_wi...  48.8 us
    pallas_call x1, Pallas kernels, body(): pl.pallas_call(write_out, out_shape=(jax.ShapeDtypeStruct(layer_out.shape...  1.86 us

profile of v3, /device:TPU:0, one launch (start us, length us, event | category | flops | bytes accessed | tf_op | source)
XLA Modules:
  0.0 51.3 jit_solution(11661107737767646243)
XLA Ops:
  0.6 48.8 %shard_map.86 = (bf16[256,1024]{1,0:T(8,128)(2,1)}, f32[16,128]{1,0:T(8,128)}) custom-call(bf16[256,1024]{1,0:T(8,128)(2,1)} %q_hbm.1, bf16[256,1024]{1,0:T(8,128)(2,1)} %k_hbm.1, bf16[256,1024]{1,0:T(8,128)(2,1)} %v_hbm.1, f32[16,1024]{1,0:T(8,128)} %rate_ref.1, f32[16,1024]{1,0:T(8,128)} %res_ref.1, f32[1,1024]{1,0:T(1,128)} %bitcast.1, ...), custom_call_target="tpu_custom_call" | custom-call | tf_op jit(solution)/shard_map/pallas_call | solution.py:308
  49.5 1.9 %shard_map.87 = (bf16[256,1024]{1,0:T(8,128)(2,1)}, f32[16,128]{1,0:T(8,128)}) custom-call(bf16[256,1024]{1,0:T(8,128)(2,1)} %get-tuple-element.4.out_ref, f32[16,128]{1,0:T(8,128)} %get-tuple-element.5.fin_ref), custom_call_target="tpu_custom_call" | custom-call | tf_op jit(solution)/shard_map/pallas_call | solution.py:347
